TPU v7x, 32 devices: a whole 2x2x4 slice. The times are simulated.
32 devices in a mesh: ep: 16 (over z, x, core), tp: 2 (over y).
Axes of the slice: x: 2, y: 2, z: 4, core: 2. Of those that a mesh axis runs over, the one named last changes fastest.
Arguments:
- tokens: bfloat16 [512, 7168], P('ep', 'tp'), may hold values from -6 to 6
- routes: int32 [512, 8], P('ep'), may hold values from 0 to 15, all different within a row; in each aligned block of 32 rows (0 to 31, 32 to 63, ...) at most 32 rows name the same one
- route_weights: float32 [512, 8], P('ep'), may hold values from 0.05 to 1
- gate_proj: bfloat16 [16, 7168, 1024], P('ep', None, 'tp'), may hold values from -0.0625 to 0.0625
- up_proj: bfloat16 [16, 7168, 1024], P('ep', None, 'tp'), may hold values from -0.0625 to 0.0625
- down_proj: bfloat16 [16, 1024, 7168], P('ep', 'tp'), may hold values from -0.1875 to 0.1875
Outputs:
- mixed: bfloat16 [512, 7168], P('ep', 'tp')
Inputs may be any that keep to these rules, and one draw needn't show every extreme that they name: `routes`: each token names 8 different experts; among the 32 tokens of one index of ep no expert is named more than 32 times.
All inputs are finite; a program needn't handle non-finite values.
Results may differ from a plain program's by a relative error of at most 0.012.
Values may be sent and summed in bfloat16 or wider, within the bound.
A program may use at most 64 MiB of HBM per device.

v0:
```python
import jax
import jax.numpy as jnp
from jax import lax
from jax.sharding import PartitionSpec as P


def per_device(tokens, routes, route_weights, gate_proj, up_proj, down_proj):
    w_gate = gate_proj[0]
    w_up = up_proj[0]
    w_down = down_proj[0]
    tok_count = tokens.shape[0]
    fanout = routes.shape[1]
    experts = lax.axis_size("ep")
    capacity = min(tok_count, max(2, 2 * tok_count * fanout // experts))
    slot_count = experts * capacity
    flat_ids = routes.reshape(-1)
    onehot = (flat_ids[:, None] == jnp.arange(experts, dtype=jnp.int32)[None, :]).astype(jnp.int32)
    before = jnp.cumsum(onehot, axis=0) - onehot
    position = jnp.sum(before * onehot, axis=1)
    target = flat_ids * capacity + position
    select = jnp.any(
        target.reshape(tok_count, fanout)[None, :, :]
        == jnp.arange(slot_count, dtype=jnp.int32)[:, None, None],
        axis=2,
    ).astype(jnp.bfloat16)
    whole = lax.all_gather(tokens, "tp", axis=1, tiled=True)
    sending = jnp.dot(select, whole, preferred_element_type=jnp.float32).astype(jnp.bfloat16)
    arrived = lax.all_to_all(sending, "ep", split_axis=0, concat_axis=0, tiled=True)
    gate_act = jnp.dot(arrived, w_gate, preferred_element_type=jnp.float32)
    up_act = jnp.dot(arrived, w_up, preferred_element_type=jnp.float32)
    hidden = (jax.nn.silu(gate_act) * up_act).astype(jnp.bfloat16)
    partial_value = jnp.dot(hidden, w_down, preferred_element_type=jnp.float32)
    summed = lax.psum_scatter(
        partial_value.astype(jnp.bfloat16), "tp", scatter_dimension=1, tiled=True
    )
    back_rows = lax.all_to_all(summed, "ep", split_axis=0, concat_axis=0, tiled=True)
    picked = jnp.take(back_rows, target, axis=0).astype(jnp.float32)
    weighted = picked * route_weights.reshape(-1)[:, None]
    mixed = jnp.sum(weighted.reshape(tok_count, fanout, -1), axis=1)
    return mixed.astype(jnp.bfloat16)


def solution(mesh):
    in_specs = (
        P("ep", "tp"),
        P("ep", None),
        P("ep", None),
        P("ep", None, "tp"),
        P("ep", None, "tp"),
        P("ep", "tp", None),
    )
    out_specs = P("ep", "tp")
    return jax.shard_map(
        per_device, mesh=mesh, in_specs=in_specs, out_specs=out_specs, check_vma=False
    )
```

profile of v0, /device:TPU:11, one launch (start us, length us, event | category | flops | bytes accessed | tf_op | source)
XLA Modules:
  0.0 391.1 jit_solution(6744728250491231129)
XLA Ops:
  6.5 0.0 reduce-scatter.2.cloned.1.call-start
  6.5 0.8 copy.15
  7.3 0.1 eq.39
  7.4 0.1 reshape.78
  7.5 0.6 reduce-window.6
  8.1 0.2 slice_reduce_fusion
  8.3 0.1 fusion.14
  8.4 0.1 reduce_sum.23
  8.5 0.2 fusion.11
  8.8 7.4 %all_gather.3 = bf16[32,7168]{1,0:T(8,128)(2,1)S(1)} all-gather(bf16[32,3584]{1,0:T(8,128)(2,1)} %param.6), channel_id=1, replica_groups=mesh['ep'=16,'tp'=2] {'tp'}, dimensions={1}, use_global_device_ids=true | all-gather | bytes 688128 | tf_op jit(solution)/shard_map/all_gather | solution.py:26
  16.1 0.0 slice-start
  16.1 2.1 convolution_convert_fusion.1
  18.2 0.0 slice-start.1
  18.2 0.0 slice-start.2
  18.3 0.0 slice-start.4
  18.3 167.1 %all_to_all.24 = bf16[16,32,7168]{2,1,0:T(8,128)(2,1)S(1)} all-to-all(bf16[16,32,7168]{2,1,0:T(8,128)(2,1)S(1)} %bitcast.47), channel_id=1, replica_groups=mesh['ep'=16,'tp'=2] {'ep'}, dimensions={0} | all-to-all | bytes 14680064 | tf_op jit(solution)/shard_map/all_to_all | solution.py:28
  185.3 0.0 slice-done
  185.3 0.0 slice-done.1
  185.3 0.0 slice-start.3
  185.3 0.0 slice-start.5
  185.4 3.9 %fusion.3 = f32[512,512]{1,0:T(8,128)S(1)} fusion(bf16[512,7168]{1,0:T(8,128)(2,1)S(1)} %bitcast.48, bf16[1,7168,512]{2,1,0:T(8,128)(2,1)S(1)} %bitcast.54), kind=kOutput, calls=%fused_computation.6 | convolution fusion | flops 3758096384 | bytes 15728640 | tf_op jit(solution)/shard_map/dot_general | solution.py:29
  189.3 0.0 slice-done.2
  189.3 0.0 slice-done.3
  189.3 4.0 %fusion.8 = bf16[512,512]{1,0:T(8,128)(2,1)S(1)} fusion(bf16[512,7168]{1,0:T(8,128)(2,1)S(1)} %bitcast.49, bf16[1,7168,512]{2,1,0:T(8,128)(2,1)S(1)} %bitcast.56, f32[512,512]{1,0:T(8,128)S(1)} %fusion.3), kind=kOutput, calls=%fused_computation.11 | convolution fusion | flops 3759669248 | bytes 16252928 | tf_op jit(solution)/shard_map/dot_general | solution.py:30
  193.4 0.0 slice-done.4
  193.4 0.0 slice-done.5
  193.4 6.0 %convolution_convert_fusion = bf16[512,7168]{1,0:T(8,128)(2,1)} fusion(bf16[512,512]{1,0:T(8,128)(2,1)S(1)} %fusion.8, bf16[1,512,7168]{2,1,0:T(8,128)(2,1)S(1)} %bitcast.58), kind=kOutput, calls=%fused_computation.1 | convolution fusion | flops 3761766400 | bytes 15204352 | tf_op jit(solution)/shard_map/dot_general | solution.py:32
  199.4 0.0 copy-start
  199.4 0.0 reduce-scatter.2.cloned.1.call-update
  199.5 88.7 %reduce-scatter.2.cloned.1.call-done = bf16[512,3584]{1,0:T(8,128)(2,1)} async-done(((bf16[512,7168]{1,0:T(8,128)(2,1)}), bf16[512,3584]{1,0:T(8,128)(2,1)}) %reduce-scatter.2.cloned.1.call-update) | async-done | bytes 3670032 | tf_op jit(solution)/shard_map/reduce_scatter | solution.py:33
  288.1 6.5 %all-to-all-start.1 = ((bf16[16,32,3584]{2,1,0:T(8,128)(2,1)}), bf16[16,32,3584]{2,1,0:T(8,128)(2,1)}, u32[]{:S(2)}, u32[]{:S(2)}) async-start(bf16[16,32,3584]{2,1,0:T(8,128)(2,1)} %bitcast.50), calls=%async_computation.2 | async-start | bytes 7340032 | tf_op jit(solution)/shard_map/all_to_all | solution.py:36
  294.6 0.1 mul.45
  294.7 0.0 copy-done
  294.7 0.1 copy.19
  294.8 81.0 %all-to-all-done.1 = bf16[16,32,3584]{2,1,0:T(8,128)(2,1)} async-done(((bf16[16,32,3584]{2,1,0:T(8,128)(2,1)}), bf16[16,32,3584]{2,1,0:T(8,128)(2,1)}, u32[]{:S(2)}, u32[]{:S(2)}) %all-to-all-start.1) | async-done | bytes 3670048 | tf_op jit(solution)/shard_map/all_to_all | solution.py:36
  375.9 6.0 %gather_fusion = bf16[256,3584]{1,0:T(8,128)(2,1)S(1)} fusion(bf16[512,3584]{1,0:T(8,128)(2,1)} %bitcast.7, s32[1024]{0:T(1024)S(1)} %pad_clamp_fusion), kind=kCustom, calls=%fused_computation | custom fusion | bytes 3671040 | tf_op jit(solution)/shard_map/jit(_take)/gather | solution.py:37
  381.9 2.4 multiply_reduce_fusion
  (10 shorter events, 0.1 us)
Async XLA Ops:
  6.5 281.6 %reduce-scatter.2.cloned.1.call-start = ((), (), s32[]{:S(2)}) async-start(), calls=%async_computation.3 | async-start | bytes 11010048 | tf_op jit(solution)/shard_map/reduce_scatter | solution.py:33
  16.1 169.2 %slice-start = ((s8[7340032]{0:T(1024)(128)(4,1)}), s8[4194304]{0:T(1024)(128)(4,1)S(1)}, s32[]{:S(2)}) async-start(s8[7340032]{0:T(1024)(128)(4,1)} %bitcast.53), calls=%async_computation.4 | async-start | bytes 8388608
  18.2 167.1 %slice-start.1 = ((s8[7340032]{0:T(1024)(128)(4,1)}), s8[3145728]{0:T(1024)(128)(4,1)S(1)}, s32[]{:S(2)}) async-start(s8[7340032]{0:T(1024)(128)(4,1)} %bitcast.53), calls=%async_computation.5 | async-start | bytes 6291456
  18.2 171.1 %slice-start.2 = ((s8[7340032]{0:T(1024)(128)(4,1)}), s8[4194304]{0:T(1024)(128)(4,1)S(1)}, s32[]{:S(2)}) async-start(s8[7340032]{0:T(1024)(128)(4,1)} %bitcast.55), calls=%async_computation.6 | async-start | bytes 8388608
  18.3 175.1 %slice-start.4 = ((s8[7340032]{0:T(1024)(128)(4,1)}), s8[3145728]{0:T(1024)(128)(4,1)S(1)}, s32[]{:S(2)}) async-start(s8[7340032]{0:T(1024)(128)(4,1)} %bitcast.57), calls=%async_computation.8 | async-start | bytes 6291456
  185.3 4.0 %slice-start.3 = ((s8[7340032]{0:T(1024)(128)(4,1)}), s8[3145728]{0:T(1024)(128)(4,1)S(1)}, s32[]{:S(2)}) async-start(s8[7340032]{0:T(1024)(128)(4,1)} %bitcast.55), calls=%async_computation.7 | async-start | bytes 6291456
  185.3 8.0 %slice-start.5 = ((s8[7340032]{0:T(1024)(128)(4,1)}), s8[4194304]{0:T(1024)(128)(4,1)S(1)}, s32[]{:S(2)}) async-start(s8[7340032]{0:T(1024)(128)(4,1)} %bitcast.57), calls=%async_computation.9 | async-start | bytes 8388608
  199.4 95.3 %copy-start = (f32[32,8]{0,1:T(8,128)S(1)}, f32[32,8]{0,1:T(8,128)}, u32[]{:S(2)}) copy-start(f32[32,8]{0,1:T(8,128)} %param.8) | copy-start | bytes 3076
  288.1 87.7 %all-to-all-start.1 = ((bf16[16,32,3584]{2,1,0:T(8,128)(2,1)}), bf16[16,32,3584]{2,1,0:T(8,128)(2,1)}, u32[]{:S(2)}, u32[]{:S(2)}) async-start(bf16[16,32,3584]{2,1,0:T(8,128)(2,1)} %bitcast.50), calls=%async_computation.2 | async-start | bytes 7340032 | tf_op jit(solution)/shard_map/all_to_all | solution.py:36
Sparse Core Ops, SparseCore 0:
  199.6 88.5 reduce-scatter.1
where the time goes:
time: 391 us
  blocking collectives  174 us (45%)
  waiting for transfers between devices  170 us (43%)
  matrix products  16.1 us (4%)
  between operations  13.5 us (3%)
  local copies, waits for them, and re-layouts  7.46 us (2%)
  starting transfers between devices  6.5 us (2%)
    all_to_all x1, blocking collectives, per_device(): lax.all_to_all(sending, 'ep', split_axis=0, concat_axis=0, tiled=True)  167 us
    reduce_scatter x1, waiting for transfers between devices, per_device(): lax.psum_scatter(partial_value.astype(jnp.bfloat16), 'tp', scatter_dimens...  88.7 us
    all_to_all x1, waiting for transfers between devices, per_device(): lax.all_to_all(summed, 'ep', split_axis=0, concat_axis=0, tiled=True)  81 us
  transfers between devices with their start and end apart: 2, of which 2 were waited for; matrix products, arithmetic and copies ran while one was open for 0% of the time, Pallas kernels for 0%

commit v1 on v0

--- a/solution.py
+++ b/solution.py
@@ -4,14 +4,13 @@
 from jax.sharding import PartitionSpec as P
 
 
-def per_device(tokens, routes, route_weights, gate_proj, up_proj, down_proj):
+def by_slots(tokens, routes, route_weights, gate_proj, up_proj, down_proj, capacity):
     w_gate = gate_proj[0]
     w_up = up_proj[0]
     w_down = down_proj[0]
     tok_count = tokens.shape[0]
     fanout = routes.shape[1]
     experts = lax.axis_size("ep")
-    capacity = min(tok_count, max(2, 2 * tok_count * fanout // experts))
     slot_count = experts * capacity
     flat_ids = routes.reshape(-1)
     onehot = (flat_ids[:, None] == jnp.arange(experts, dtype=jnp.int32)[None, :]).astype(jnp.int32)
@@ -40,6 +39,31 @@
     return mixed.astype(jnp.bfloat16)
 
 
+def by_tokens(tokens, routes, route_weights, gate_proj, up_proj, down_proj):
+    experts = lax.axis_size("ep")
+    chosen = routes[:, :, None] == jnp.arange(experts, dtype=jnp.int32)
+    dense = jnp.sum(jnp.where(chosen, route_weights[:, :, None], 0.0), axis=1)
+    mine = lax.all_to_all(dense.T, "ep", split_axis=0, concat_axis=0, tiled=True).reshape(-1)
+    half = lax.all_gather(tokens, "ep", axis=0, tiled=True)
+    rows = lax.all_gather(half, "tp", axis=1, tiled=True)
+    gate_act = jnp.dot(rows, gate_proj[0], preferred_element_type=jnp.float32)
+    up_act = jnp.dot(rows, up_proj[0], preferred_element_type=jnp.float32)
+    hidden = (jax.nn.silu(gate_act) * up_act * mine[:, None]).astype(jnp.bfloat16)
+    partial_value = jnp.dot(hidden, down_proj[0], preferred_element_type=jnp.float32)
+    summed = lax.psum_scatter(
+        partial_value.astype(jnp.bfloat16), "tp", scatter_dimension=1, tiled=True
+    )
+    return lax.psum_scatter(summed, "ep", scatter_dimension=0, tiled=True)
+
+
+def per_device(tokens, routes, *rest):
+    tok_count = tokens.shape[0]
+    capacity = min(tok_count, max(2, 2 * tok_count * routes.shape[1] // lax.axis_size("ep")))
+    if capacity == tok_count:
+        return by_tokens(tokens, routes, *rest)
+    return by_slots(tokens, routes, *rest, capacity)
+
+
 def solution(mesh):
     in_specs = (
         P("ep", "tp"),

time: 391 us -> 343 us (0.88)
  the two profiles are of different devices: /device:TPU:11 before, /device:TPU:0 now
where the time goes in v1:
time: 343 us
  waiting for transfers between devices  295 us (86%)
  matrix products  22.6 us (7%)
  between operations  13.2 us (4%)
  blocking collectives  9.65 us (3%)
    reduce_scatter x1, waiting for transfers between devices, by_tokens(): lax.psum_scatter(partial_value.astype(jnp.bfloat16), 'tp', scatter_dimens...  88.6 us
    all_gather x1, waiting for transfers between devices, by_tokens(): rows = lax.all_gather(half, 'tp', axis=1, tiled=True)  80.7 us
    reduce_scatter x1, waiting for transfers between devices, by_tokens(): return lax.psum_scatter(summed, 'ep', scatter_dimension=0, tiled=True)  72.3 us
    all_gather x1, waiting for transfers between devices, by_tokens(): half = lax.all_gather(tokens, 'ep', axis=0, tiled=True)  52.7 us
    all_to_all x1, blocking collectives, by_tokens(): lax.all_to_all(dense.T, 'ep', split_axis=0, concat_axis=0, tiled=True)  9.65 us
    dot_general x1, matrix products, by_tokens(): gate_act = jnp.dot(rows, gate_proj[0], preferred_element_type=jnp.float32)  9.21 us
    dot_general x1, matrix products, by_tokens(): up_act = jnp.dot(rows, up_proj[0], preferred_element_type=jnp.float32)  7.35 us
  transfers between devices with their start and end apart: 4, of which 4 were waited for; matrix products, arithmetic and copies ran while one was open for 1% of the time, Pallas kernels for 0%

profile of v1, /device:TPU:0, one launch (start us, length us, event | category | flops | bytes accessed | tf_op | source)
XLA Modules:
  0.0 342.6 jit_solution(661104241288667825)
XLA Ops:
  6.5 0.0 all-gather.3.cloned.1.call-start
  6.5 0.7 all-gather.3.cloned.1.call-update
  7.3 0.0 all-gather.5.cloned.1.call-start
  7.3 52.7 %all-gather.3.cloned.1.call-done = bf16[512,3584]{1,0:T(8,128)(2,1)} async-done(((bf16[32,3584]{1,0:T(8,128)(2,1)}), bf16[512,3584]{1,0:T(8,128)(2,1)}) %all-gather.3.cloned.1.call-update) | async-done | bytes 3670032 | tf_op jit(solution)/shard_map/all_gather | solution.py:47
  60.0 0.0 all-gather.5.cloned.1.call-update
  60.0 0.0 reduce-scatter.3.cloned.1.call-start
  60.1 0.7 select_reduce_fusion
  60.8 9.7 %all_to_all.9 = f32[16,1,32]{2,1,0:T(1,128)S(1)} all-to-all(f32[16,1,32]{2,1,0:T(1,128)S(1)} %bitcast.23), channel_id=1, replica_groups=mesh['ep'=16,'tp'=2] {'ep'}, dimensions={0} | all-to-all | bytes 4096 | tf_op jit(solution)/shard_map/all_to_all | solution.py:46
  70.5 0.5 broadcast.7
  71.0 0.7 reduce.3
  71.7 0.1 mul.19
  71.7 80.7 %all-gather.5.cloned.1.call-done = bf16[512,7168]{1,0:T(8,128)(2,1)} async-done(((bf16[512,3584]{1,0:T(8,128)(2,1)}), bf16[512,7168]{1,0:T(8,128)(2,1)}) %all-gather.5.cloned.1.call-update) | async-done | bytes 7340048 | tf_op jit(solution)/shard_map/all_gather | solution.py:48
  152.5 0.0 copy-start.1
  152.5 9.2 %fusion.3 = f32[512,512]{1,0:T(8,128)S(1)} fusion(bf16[512,7168]{1,0:T(8,128)(2,1)} %all-gather.5.cloned.1.call-done, bf16[1,7168,512]{2,1,0:T(8,128)(2,1)} %param.9), kind=kOutput, calls=%fused_computation.4 | convolution fusion | flops 3758096384 | bytes 15728640 | tf_op jit(solution)/shard_map/dot_general | solution.py:49
  161.7 0.0 copy-done.1
  161.7 0.0 copy-start
  161.7 7.4 %fusion.11 = bf16[512,512]{1,0:T(8,128)(2,1)S(1)} fusion(bf16[512,7168]{1,0:T(8,128)(2,1)S(1)} %copy-done.1, bf16[1,7168,512]{2,1,0:T(8,128)(2,1)} %param.10, f32[512,512]{1,0:T(8,128)S(1)} %fusion.3, f32[512]{0:T(512)S(1)} %mul.19), kind=kOutput, calls=%fused_computation.8 | convolution fusion | flops 3759931392 | bytes 16254976 | tf_op jit(solution)/shard_map/dot_general | solution.py:50
  169.1 0.0 copy-done
  169.1 6.0 %convolution_convert_fusion = bf16[512,7168]{1,0:T(8,128)(2,1)} fusion(bf16[512,512]{1,0:T(8,128)(2,1)S(1)} %fusion.11, bf16[1,512,7168]{2,1,0:T(8,128)(2,1)S(1)} %copy-done), kind=kOutput, calls=%fused_computation | convolution fusion | flops 3761766400 | bytes 15204352 | tf_op jit(solution)/shard_map/dot_general | solution.py:52
  175.1 0.0 reduce-scatter.3.cloned.1.call-update
  175.1 0.0 reduce-scatter.5.cloned.1.call-start
  175.2 88.6 %reduce-scatter.3.cloned.1.call-done = bf16[512,3584]{1,0:T(8,128)(2,1)} async-done(((bf16[512,7168]{1,0:T(8,128)(2,1)}), bf16[512,3584]{1,0:T(8,128)(2,1)}) %reduce-scatter.3.cloned.1.call-update) | async-done | bytes 3670032 | tf_op jit(solution)/shard_map/reduce_scatter | solution.py:53
  263.8 0.0 reduce-scatter.5.cloned.1.call-update
  263.8 72.3 %reduce-scatter.5.cloned.1.call-done = bf16[32,3584]{1,0:T(8,128)(2,1)} async-done(((bf16[512,3584]{1,0:T(8,128)(2,1)}), bf16[32,3584]{1,0:T(8,128)(2,1)}) %reduce-scatter.5.cloned.1.call-update) | async-done | bytes 229392 | tf_op jit(solution)/shard_map/reduce_scatter | solution.py:56
Async XLA Ops:
  6.5 53.5 %all-gather.3.cloned.1.call-start = ((), (), s32[]{:S(2)}) async-start(), calls=%async_computation.3 | async-start | bytes 3899392 | tf_op jit(solution)/shard_map/all_gather | solution.py:47
  7.3 145.2 %all-gather.5.cloned.1.call-start = ((), (), s32[]{:S(2)}) async-start(), calls=%async_computation.4 | async-start | bytes 11010048 | tf_op jit(solution)/shard_map/all_gather | solution.py:48
  60.0 203.8 %reduce-scatter.3.cloned.1.call-start = ((), (), s32[]{:S(2)}) async-start(), calls=%async_computation.5 | async-start | bytes 11010048 | tf_op jit(solution)/shard_map/reduce_scatter | solution.py:53
  152.5 9.2 %copy-start.1 = (bf16[512,7168]{1,0:T(8,128)(2,1)S(1)}, bf16[512,7168]{1,0:T(8,128)(2,1)}, u32[]{:S(2)}) copy-start(bf16[512,7168]{1,0:T(8,128)(2,1)} %all-gather.5.cloned.1.call-done) | copy-start | bytes 22020100
  161.7 7.4 %copy-start = (bf16[1,512,7168]{2,1,0:T(8,128)(2,1)S(1)}, bf16[1,512,7168]{2,1,0:T(8,128)(2,1)}, u32[]{:S(2)}) copy-start(bf16[1,512,7168]{2,1,0:T(8,128)(2,1)} %param.11) | copy-start | bytes 22020100
  175.1 161.0 %reduce-scatter.5.cloned.1.call-start = ((), (), s32[]{:S(2)}) async-start(), calls=%async_computation.6 | async-start | bytes 3899392 | tf_op jit(solution)/shard_map/reduce_scatter | solution.py:56
Sparse Core Ops, SparseCore 0:
  9.6 50.3 all-gather.2
  61.6 90.8 all-gather.4
  175.3 88.5 reduce-scatter.2
  267.5 68.5 reduce-scatter.4

commit v2 on v1

--- a/solution.py
+++ b/solution.py
@@ -1,6 +1,12 @@
+import functools
+import heapq
+import itertools
+
 import jax
 import jax.numpy as jnp
 from jax import lax
+from jax.experimental import pallas as pl
+from jax.experimental.pallas import tpu as pltpu
 from jax.sharding import PartitionSpec as P
 
 
@@ -39,27 +45,336 @@
     return mixed.astype(jnp.bfloat16)
 
 
+LINK = 46e3
+PAIR = 150e3
+
+
+def edges(order, block, ring):
+    place = dict(zip("zxy", block))
+    stage = max([i for i, axis in enumerate(order) if place[axis]], default=-1)
+    out = []
+    for i in range(max(stage, 0), len(order)):
+        axis = order[i]
+        limit = ring - 1 if axis == "z" else 1
+        if place[axis] < limit:
+            out.append((axis, tuple(place[a] + (a == axis) for a in "zxy")))
+    return out
+
+
+def make_plan(parts, ring, rows, gate_us, down_us):
+    heap, ops, count, free = [], [], itertools.count(), {}
+    clock = 0.0
+
+    def push(time, *event):
+        heapq.heappush(heap, (time, next(count), event))
+
+    def send(link, size, rate, delay):
+        free[link] = max(clock, free.get(link, 0.0)) + size / rate
+        return free[link] + delay
+
+    held, finished, made, got = {}, {}, {}, {}
+    blocks = [(z, x, y) for z in range(ring) for x in range(2) for y in range(2)]
+    children = {(p, b): [c for _, c in edges(order, b, ring)] for p, (order, _, _) in enumerate(parts) for b in blocks}
+    parent = {(p, c): b for (p, b), cs in children.items() for c in cs}
+
+    def hold(block):
+        key = (block[0], block[2])
+        held[key] = held.get(key, 0) + 1
+        if held[key] == 4 * len(parts):
+            push(clock, "gate", *key)
+
+    def reach(p, block):
+        got[p, block] = got.get((p, block), 0) + 1
+        if got[p, block] == 1 + len(children[p, block]):
+            push(clock, "sum", p, block)
+
+    for p in range(len(parts)):
+        push(0.0, "have", p, (0, 0, 0))
+    while heap:
+        time, _, event = heapq.heappop(heap)
+        clock = max(clock, time)
+        ops.append(event)
+        kind = event[0]
+        if kind == "have":
+            _, p, block = event
+            order, _, width = parts[p]
+            for axis, child in edges(order, block, ring):
+                push(send(axis, rows * width * 2, LINK, 1.6), "have", p, child)
+            push(send("core", rows * width * 2, PAIR, 0.9), "mate", p, block)
+            hold(block)
+        elif kind == "mate":
+            hold(event[2])
+        elif kind == "gate":
+            clock += gate_us
+            finished[event[1]] = finished.get(event[1], 0) + 1
+            if finished[event[1]] == 2:
+                for y in (1, 0):
+                    push(clock, "down", event[1], y)
+        elif kind == "down":
+            clock += down_us
+            width = sum(part[2] for part in parts)
+            for x in (1, 0):
+                push(send("core", rows * width * 2, PAIR, 0.9), "back", (event[1], x, event[2]))
+        elif kind == "back":
+            for p in range(len(parts)):
+                reach(p, event[1])
+        elif kind == "sum":
+            _, p, block = event
+            clock += 0.1
+            if (p, block) in parent:
+                axis = [a for a, i, j in zip("zxy", block, parent[p, block]) if i != j][0]
+                push(send(axis, rows * parts[p][2] * 2, LINK, 1.6), "came", p, block)
+        elif kind == "came":
+            reach(event[1], parent[event[1], event[2]])
+    return ops, children, parent
+
+
+def layer_kernel(parts, ring, plan, tokens, shares, gate_hbm, up_hbm, down_hbm, out, everything, w_gate, w_up, w_down,
+                 gate_acc, up_acc, hidden, result, mate_rows, landed, weights, own_sem, load_sem, have_send, have_recv,
+                 mate_send, mate_recv, back_send, back_recv, sum_send, sum_recv, share_send, share_recv):
+    ops, children, parent = plan
+    ep, tp = lax.axis_index("ep"), lax.axis_index("tp")
+    core, side, level = lax.rem(ep, 2), lax.rem(ep // 2, 2), ep // 4
+    rows, half = tokens.shape
+    group = 4 * rows
+
+    def device(z=0, x=0, y=0, c=0):
+        new_z = lax.rem(level + z + ring, ring)
+        new_x = lax.rem(side + x, 2)
+        return (new_z * 2 + new_x) * 2 + lax.rem(core + c, 2), lax.rem(tp + y, 2)
+
+    def number(block):
+        return (block[0] * 2 + block[1]) * 2 + block[2]
+
+    def place(block, c=0):
+        return pl.ds(((block[0] * 2 + block[1]) * 2 + c) * rows, rows)
+
+    def pair_place(block):
+        return pl.ds((block[0] * 2 + block[1]) * rows, rows)
+
+    def columns(p):
+        return pl.ds(parts[p][1], parts[p][2])
+
+    def remote(src, dst, send, recv, target):
+        return pltpu.make_async_remote_copy(src_ref=src, dst_ref=dst, send_sem=send, recv_sem=recv,
+                                            device_id=target, device_id_type=pl.DeviceIdType.MESH)
+
+    def have_copy(p, child, axis):
+        block = tuple(v - (a == axis) for a, v in zip("zxy", child))
+        if block == (0, 0, 0):
+            src = tokens.at[:, columns(p)]
+        else:
+            src = everything.at[block[2], place(block), columns(p)]
+        return remote(src, everything.at[child[2], place(child), columns(p)], have_send.at[p, number(child)],
+                      have_recv.at[p, number(child)], device(**{axis: 1}))
+
+    def mate_copy(p, block):
+        if block == (0, 0, 0):
+            src = tokens.at[:, columns(p)]
+        else:
+            src = everything.at[block[2], place(block), columns(p)]
+        return remote(src, everything.at[block[2], place(block, 1), columns(p)], mate_send.at[p, number(block)],
+                      mate_recv.at[p, number(block)], device(c=1))
+
+    def back_copy(block):
+        return remote(result.at[block[2], place(block, 1)], mate_rows.at[block[2], pair_place(block)],
+                      back_send.at[number(block)], back_recv.at[number(block)], device(c=1))
+
+    def sum_copy(p, block):
+        axis = [a for a, i, j in zip("zxy", block, parent[p, block]) if i != j][0]
+        return remote(result.at[block[2], place(block), columns(p)], landed.at[block[2], pair_place(block), columns(p)],
+                      sum_send.at[p, number(block)], sum_recv.at[p, number(block)], device(**{axis: -1 if axis == "z" else 1}))
+
+    peers = [(z, x, c) for z in range(ring) for x in range(2) for c in range(2) if (z, x, c) != (0, 0, 0)]
+
+    def share_copy(peer):
+        z, x, c = peer
+        target = device(z=z, x=x, c=c)
+        i = number(peer)
+        return remote(shares.at[target[0]], weights.at[i], share_send.at[i], share_recv.at[i], target)
+
+    loads = []
+    for y in range(2):
+        at = lax.rem(tp + y, 2) * half
+        loads.append([
+            pltpu.make_async_copy(gate_hbm.at[pl.ds(at, half)], w_gate.at[y], load_sem.at[y, 0]),
+            pltpu.make_async_copy(up_hbm.at[pl.ds(at, half)], w_up.at[y], load_sem.at[y, 1]),
+            pltpu.make_async_copy(down_hbm.at[:, pl.ds(pl.multiple_of(at, 128), half)], w_down.at[y], load_sem.at[y, 2]),
+        ])
+    own = pltpu.make_async_copy(tokens, everything.at[0, pl.ds(0, rows)], own_sem)
+    own_share = pltpu.make_async_copy(shares.at[ep], weights.at[0], share_send.at[0])
+
+    own.start()
+    own_share.start()
+    for kind in ((0, 1), (2,)):
+        for y in range(2):
+            for i in kind:
+                loads[y][i].start()
+    barrier = pltpu.get_barrier_semaphore()
+    greeted = [device(z=z, x=x, c=c) for z, x, c in peers] + [device(y=1)]
+    for target in greeted:
+        pl.semaphore_signal(barrier, inc=1, device_id=target, device_id_type=pl.DeviceIdType.MESH)
+    pl.semaphore_wait(barrier, len(greeted))
+    for peer in peers:
+        share_copy(peer).start()
+
+    waited = set()
+
+    def once(key, copy):
+        if key not in waited:
+            waited.add(key)
+            copy.wait()
+
+    def gate(z, y, first, last):
+        once("own", own)
+        once(("load", y, 0), loads[y][0])
+        once(("load", y, 1), loads[y][1])
+        here = pl.ds(z * group, group)
+        tile = 512 if half % 512 == 0 else 128
+        if first:
+            gate_acc[here] = jnp.zeros((group, gate_acc.shape[1]), jnp.float32)
+            up_acc[here] = jnp.zeros((group, gate_acc.shape[1]), jnp.float32)
+
+        def step(k, carry):
+            depth = pl.ds(pl.multiple_of(k * tile, tile), tile)
+            x = everything[y, here, depth]
+            gate_acc[here] += jnp.dot(x, w_gate[y, depth], preferred_element_type=jnp.float32)
+            up_acc[here] += jnp.dot(x, w_up[y, depth], preferred_element_type=jnp.float32)
+            return carry
+
+        lax.fori_loop(0, half // tile, step, 0)
+        if last:
+            for x in range(2):
+                for c in range(2):
+                    i = number((z, x, c))
+                    if i:
+                        share_copy((z, x, c)).wait_recv()
+                    else:
+                        own_share.wait()
+                    row = lax.broadcasted_iota(jnp.int32, (rows, 128), 0)
+                    lane = lax.broadcasted_iota(jnp.int32, (rows, 128), 1)
+                    spread = jnp.broadcast_to(weights[i, 0:1, :], (rows, 128))
+                    weight = jnp.sum(jnp.where(row == lane, spread, 0.0), axis=1, keepdims=True)
+                    at = pl.ds(i * rows, rows)
+                    g = gate_acc[at]
+                    hidden[at] = (g / (1.0 + jnp.exp(-g)) * up_acc[at] * weight).astype(hidden.dtype)
+
+    def down(z, y):
+        once(("load", y, 2), loads[y][2])
+        here = pl.ds(z * group, group)
+        tile = 512 if half % 512 == 0 else 128
+
+        def step(k, carry):
+            across = pl.ds(pl.multiple_of(k * tile, tile), tile)
+            result[y, here, across] = jnp.dot(
+                hidden[here], w_down[y, :, across], preferred_element_type=jnp.float32).astype(result.dtype)
+            return carry
+
+        lax.fori_loop(0, half // tile, step, 0)
+
+    gates, sent = {}, []
+    for event in ops:
+        kind = event[0]
+        if kind == "have":
+            _, p, block = event
+            if block != (0, 0, 0):
+                axis = [a for a, i, j in zip("zxy", block, parent[p, block]) if i != j][0]
+                have_copy(p, block, axis).wait_recv()
+            for axis, child in edges(parts[p][0], block, ring):
+                have_copy(p, child, axis).start()
+                sent.append(have_copy(p, child, axis))
+            mate_copy(p, block).start()
+            sent.append(mate_copy(p, block))
+        elif kind == "mate":
+            mate_copy(event[1], event[2]).wait_recv()
+        elif kind == "gate":
+            z, y = event[1:]
+            gates[z] = gates.get(z, 0) + 1
+            gate(z, y, gates[z] == 1, gates[z] == 2)
+        elif kind == "down":
+            z, y = event[1:]
+            down(z, y)
+            for x in (1, 0):
+                back_copy((z, x, y)).start()
+                sent.append(back_copy((z, x, y)))
+        elif kind == "back":
+            back_copy(event[1]).wait_recv()
+        elif kind == "came":
+            sum_copy(event[1], event[2]).wait_recv()
+        elif kind == "sum":
+            _, p, block = event
+            y = block[2]
+            total = result[y, place(block), columns(p)].astype(jnp.float32)
+            total += mate_rows[y, pair_place(block), columns(p)].astype(jnp.float32)
+            for child in children[p, block]:
+                total += landed[child[2], pair_place(child), columns(p)].astype(jnp.float32)
+            if (p, block) in parent:
+                result[y, place(block), columns(p)] = total.astype(result.dtype)
+                sum_copy(p, block).start()
+                sent.append(sum_copy(p, block))
+            else:
+                out[:, columns(p)] = total.astype(out.dtype)
+    for copy in sent:
+        copy.wait_send()
+    for peer in peers:
+        share_copy(peer).wait_send()
+
+
 def by_tokens(tokens, routes, route_weights, gate_proj, up_proj, down_proj):
     experts = lax.axis_size("ep")
+    rows, half = tokens.shape
+    depth = gate_proj.shape[2]
+    ring = experts // 4
     chosen = routes[:, :, None] == jnp.arange(experts, dtype=jnp.int32)
     dense = jnp.sum(jnp.where(chosen, route_weights[:, :, None], 0.0), axis=1)
-    mine = lax.all_to_all(dense.T, "ep", split_axis=0, concat_axis=0, tiled=True).reshape(-1)
-    half = lax.all_gather(tokens, "ep", axis=0, tiled=True)
-    rows = lax.all_gather(half, "tp", axis=1, tiled=True)
-    gate_act = jnp.dot(rows, gate_proj[0], preferred_element_type=jnp.float32)
-    up_act = jnp.dot(rows, up_proj[0], preferred_element_type=jnp.float32)
-    hidden = (jax.nn.silu(gate_act) * up_act * mine[:, None]).astype(jnp.bfloat16)
-    partial_value = jnp.dot(hidden, down_proj[0], preferred_element_type=jnp.float32)
-    summed = lax.psum_scatter(
-        partial_value.astype(jnp.bfloat16), "tp", scatter_dimension=1, tiled=True
-    )
-    return lax.psum_scatter(summed, "ep", scatter_dimension=0, tiled=True)
+    shares = jnp.pad(dense.T, ((0, 0), (0, 128 - rows)))
+    shares = jnp.broadcast_to(shares[:, None, :], (experts, 8, 128))
+    tiles = half // 128
+    most = max(1, tiles * 11 // 28)
+    widths = [tiles - 2 * most, most, most]
+    parts, at = [], 0
+    for order, width in zip(("xyz", "zxy", "zyx"), widths):
+        parts.append((order, at * 128, width * 128))
+        at += width
+    plan = make_plan(parts, ring, rows, 1.6, 0.7)
+    count, total = 4 * ring, experts * rows
+    any_space = pl.BlockSpec(memory_space=pl.ANY)
+    vmem = pl.BlockSpec(memory_space=pltpu.VMEM)
+    dma = pltpu.SemaphoreType.DMA
+    bf16, f32 = jnp.bfloat16, jnp.float32
+    return pl.pallas_call(
+        functools.partial(layer_kernel, parts, ring, plan),
+        out_shape=jax.ShapeDtypeStruct(tokens.shape, tokens.dtype),
+        in_specs=[vmem, vmem, any_space, any_space, any_space],
+        out_specs=vmem,
+        scratch_shapes=[
+            pltpu.VMEM((2, total, half), bf16),
+            pltpu.VMEM((2, half, depth), bf16),
+            pltpu.VMEM((2, half, depth), bf16),
+            pltpu.VMEM((2, depth, half), bf16),
+            pltpu.VMEM((total, depth), f32),
+            pltpu.VMEM((total, depth), f32),
+            pltpu.VMEM((total, depth), bf16),
+            pltpu.VMEM((2, total, half), bf16),
+            pltpu.VMEM((2, total // 2, half), bf16),
+            pltpu.VMEM((2, total // 2, half), bf16),
+            pltpu.VMEM((experts, 8, 128), f32),
+            dma, dma((2, 3)),
+            dma((3, count)), dma((3, count)),
+            dma((3, count)), dma((3, count)),
+            dma((count,)), dma((count,)),
+            dma((3, count)), dma((3, count)),
+            dma((experts,)), dma((experts,)),
+        ],
+        compiler_params=pltpu.CompilerParams(
+            collective_id=0, has_side_effects=True, vmem_limit_bytes=60 << 20),
+    )(tokens, shares, gate_proj[0], up_proj[0], down_proj[0])
 
 
 def per_device(tokens, routes, *rest):
     tok_count = tokens.shape[0]
     capacity = min(tok_count, max(2, 2 * tok_count * routes.shape[1] // lax.axis_size("ep")))
-    if capacity == tok_count:
+    if capacity == tok_count and tok_count % 16 == 0 and tok_count <= 128 and lax.axis_size("ep") % 4 == 0 and lax.axis_size("tp") == 2:
         return by_tokens(tokens, routes, *rest)
     return by_slots(tokens, routes, *rest, capacity)
 

time: 343 us -> 104 us (0.30)
  waiting for transfers between devices: 295 us -> 0 us
  Pallas kernels: 0 us -> 100 us
  matrix products: 22.6 us -> 0 us
  between operations: 13.2 us -> 0.02 us
  blocking collectives: 9.65 us -> 0 us
    reduce_scatter x2 -> x0, waiting for transfers between devices: 161 us -> none  [the longest x1 88.6 us: by_tokens(): lax.psum_scatter(partial_value.astype(jnp.bfloat16), 'tp', scatter_dimens...]
    all_gather x2 -> x0, waiting for transfers between devices: 133 us -> none  [the longest x1 80.7 us: by_tokens(): rows = lax.all_gather(half, 'tp', axis=1, tiled=True)]
    pallas_call x0 -> x1, Pallas kernels: none -> 100 us  [by_tokens(): pl.pallas_call(functools.partial(layer_kernel, parts, ring, plan), out_sh...]
    dot_general x3 -> x0, matrix products: 22.6 us -> none  [the longest x1 9.21 us: by_tokens(): gate_act = jnp.dot(rows, gate_proj[0], preferred_element_type=jnp.float32)]
    all_to_all x1 -> x0, blocking collectives: 9.65 us -> none  [by_tokens(): lax.all_to_all(dense.T, 'ep', split_axis=0, concat_axis=0, tiled=True)]
  transfers between devices with their start and end apart: 4 -> 0, of which waited for: 4 -> 0; matrix products, arithmetic and copies ran while one was open for 1% -> 0% of each run, Pallas kernels for 0% -> 0%
where the time goes in v2:
time: 104 us; the launch traced here: 103 us
  Pallas kernels  100 us (96%)
  local copies, waits for them, and re-layouts  2.28 us (2%)
    pallas_call x1, Pallas kernels, by_tokens(): pl.pallas_call(functools.partial(layer_kernel, parts, ring, plan), out_sh...  100 us

profile of v2, /device:TPU:0, one launch (start us, length us, event | category | flops | bytes accessed | tf_op | source)
XLA Modules:
  0.0 103.4 jit_solution(6589805180825853955)
XLA Ops:
  0.0 0.7 select_reduce_fusion
  0.7 0.6 broadcast_in_dim.23.shares
  1.4 100.4 %shard_map.64 = bf16[32,3584]{1,0:T(8,128)(2,1)} custom-call(bf16[32,3584]{1,0:T(8,128)(2,1)} %tokens.1, f32[16,8,128]{2,1,0:T(8,128)} %broadcast_in_dim.23.shares, bf16[7168,512]{1,0:T(8,128)(2,1)} %bitcast.4, bf16[7168,512]{1,0:T(8,128)(2,1)} %bitcast.5, bf16[512,7168]{1,0:T(8,128)(2,1)} %bitcast.6), custom_call_target="tpu_custom_call" | custom-call | tf_op jit(solution)/shard_map/pallas_call | solution.py:345
  101.8 1.6 %copy.10 = bf16[32,3584]{1,0:T(8,128)(2,1)} copy(bf16[32,3584]{1,0:T(8,128)(2,1)} %shard_map.64) | data formatting | bytes 458752
  (1 shorter events, 0.0 us)

commit v3 on v2

--- a/solution.py
+++ b/solution.py
@@ -45,8 +45,8 @@
     return mixed.astype(jnp.bfloat16)
 
 
-LINK = 46e3
-PAIR = 150e3
+LINK = 40e3
+PAIR = 300e3
 
 
 def edges(order, block, ring):
@@ -336,7 +336,7 @@
     for order, width in zip(("xyz", "zxy", "zyx"), widths):
         parts.append((order, at * 128, width * 128))
         at += width
-    plan = make_plan(parts, ring, rows, 1.6, 0.7)
+    plan = make_plan(parts, ring, rows, 2.0, 1.6)
     count, total = 4 * ring, experts * rows
     any_space = pl.BlockSpec(memory_space=pl.ANY)
     vmem = pl.BlockSpec(memory_space=pltpu.VMEM)

time: 104 us -> 92.1 us (0.89)
  Pallas kernels: 100 us -> 88.8 us
    pallas_call x1, Pallas kernels: 100 us -> 88.8 us  [by_tokens(): pl.pallas_call(functools.partial(layer_kernel, parts, ring, plan), out_sh...]
where the time goes in v3:
time: 92.1 us; the launch traced here: 91.9 us
  Pallas kernels  88.8 us (96%)
  local copies, waits for them, and re-layouts  2.28 us (2%)
    pallas_call x1, Pallas kernels, by_tokens(): pl.pallas_call(functools.partial(layer_kernel, parts, ring, plan), out_sh...  88.8 us

profile of v3, /device:TPU:0, one launch (start us, length us, event | category | flops | bytes accessed | tf_op | source)
XLA Modules:
  0.0 91.9 jit_solution(17985293964316291859)
XLA Ops:
  0.0 0.7 select_reduce_fusion
  0.7 0.6 broadcast_in_dim.23.shares
  1.4 88.8 %shard_map.64 = bf16[32,3584]{1,0:T(8,128)(2,1)} custom-call(bf16[32,3584]{1,0:T(8,128)(2,1)} %tokens.1, f32[16,8,128]{2,1,0:T(8,128)} %broadcast_in_dim.23.shares, bf16[7168,512]{1,0:T(8,128)(2,1)} %bitcast.4, bf16[7168,512]{1,0:T(8,128)(2,1)} %bitcast.5, bf16[512,7168]{1,0:T(8,128)(2,1)} %bitcast.6), custom_call_target="tpu_custom_call" | custom-call | tf_op jit(solution)/shard_map/pallas_call | solution.py:345
  90.2 1.6 %copy.10 = bf16[32,3584]{1,0:T(8,128)(2,1)} copy(bf16[32,3584]{1,0:T(8,128)(2,1)} %shard_map.64) | data formatting | bytes 458752
  (1 shorter events, 0.0 us)

commit v4 on v3

--- a/solution.py
+++ b/solution.py
@@ -204,16 +204,16 @@
     own = pltpu.make_async_copy(tokens, everything.at[0, pl.ds(0, rows)], own_sem)
     own_share = pltpu.make_async_copy(shares.at[ep], weights.at[0], share_send.at[0])
 
+    barrier = pltpu.get_barrier_semaphore()
+    greeted = [device(z=z, x=x, c=c) for z, x, c in peers] + [device(y=1)]
+    for target in greeted:
+        pl.semaphore_signal(barrier, inc=1, device_id=target, device_id_type=pl.DeviceIdType.MESH)
     own.start()
     own_share.start()
     for kind in ((0, 1), (2,)):
         for y in range(2):
             for i in kind:
                 loads[y][i].start()
-    barrier = pltpu.get_barrier_semaphore()
-    greeted = [device(z=z, x=x, c=c) for z, x, c in peers] + [device(y=1)]
-    for target in greeted:
-        pl.semaphore_signal(barrier, inc=1, device_id=target, device_id_type=pl.DeviceIdType.MESH)
     pl.semaphore_wait(barrier, len(greeted))
     for peer in peers:
         share_copy(peer).start()
@@ -336,7 +336,7 @@
     for order, width in zip(("xyz", "zxy", "zyx"), widths):
         parts.append((order, at * 128, width * 128))
         at += width
-    plan = make_plan(parts, ring, rows, 2.0, 1.6)
+    plan = make_plan(parts, ring, rows, 2.4, 1.6)
     count, total = 4 * ring, experts * rows
     any_space = pl.BlockSpec(memory_space=pl.ANY)
     vmem = pl.BlockSpec(memory_space=pltpu.VMEM)

time: 92.1 us -> 89.4 us (0.971)
  Pallas kernels: 88.8 us -> 86.1 us
    pallas_call x1, Pallas kernels: 88.8 us -> 86.1 us  [by_tokens(): pl.pallas_call(functools.partial(layer_kernel, parts, ring, plan), out_sh...]
where the time goes in v4:
time: 89.4 us; the launch traced here: 89.2 us
  Pallas kernels  86.1 us (96%)
  local copies, waits for them, and re-layouts  2.28 us (3%)
    pallas_call x1, Pallas kernels, by_tokens(): pl.pallas_call(functools.partial(layer_kernel, parts, ring, plan), out_sh...  86.1 us

profile of v4, /device:TPU:0, one launch (start us, length us, event | category | flops | bytes accessed | tf_op | source)
XLA Modules:
  0.0 89.2 jit_solution(2108630064419679701)
XLA Ops:
  0.0 0.7 select_reduce_fusion
  0.7 0.6 broadcast_in_dim.23.shares
  1.4 86.1 %shard_map.64 = bf16[32,3584]{1,0:T(8,128)(2,1)} custom-call(bf16[32,3584]{1,0:T(8,128)(2,1)} %tokens.1, f32[16,8,128]{2,1,0:T(8,128)} %broadcast_in_dim.23.shares, bf16[7168,512]{1,0:T(8,128)(2,1)} %bitcast.4, bf16[7168,512]{1,0:T(8,128)(2,1)} %bitcast.5, bf16[512,7168]{1,0:T(8,128)(2,1)} %bitcast.6), custom_call_target="tpu_custom_call" | custom-call | tf_op jit(solution)/shard_map/pallas_call | solution.py:345
  87.5 1.6 %copy.10 = bf16[32,3584]{1,0:T(8,128)(2,1)} copy(bf16[32,3584]{1,0:T(8,128)(2,1)} %shard_map.64) | data formatting | bytes 458752
  (1 shorter events, 0.0 us)
